TPU v7x, 512 devices: a whole 4x8x8 slice. The times are simulated.
512 devices in a mesh: batch: 8 (over y), grp: 64 (over x, z, core).
Axes of the slice: x: 4, y: 8, z: 8, core: 2. Of those that a mesh axis runs over, the one named last changes fastest.
Arguments:
- amps: bfloat16 [24, 64, 1024, 128], P('batch', None, 'grp'), may hold values from -6 to 6
- cycle_inter: bfloat16 [24, 1024, 8, 128], P('batch', 'grp'), may hold values from -0.109375 to 0.109375
- k_irrep: int32 [24], replicated, may hold values from 0 to 7
- i_irrep: int32 [64], replicated, may hold values from 0 to 7
- j_irrep: int32 [8], replicated, may hold values from 0 to 7
- virt_count: int32 [8], replicated, may hold values from 64 to 128, as said below
Outputs:
- cycle_term: bfloat16 [64, 8, 1024, 128], P(None, 'batch', 'grp')
Inputs may be any that keep to these rules, and one draw needn't show every extreme that they name: `virt_count`: together the counts are 800.
All inputs are finite; a program needn't handle non-finite values.
Results may differ from a plain program's by a relative error of at most 0.013.
Values may be sent and summed in bfloat16 or wider, within the bound.
A program may use at most 64 MiB of HBM per device.

v0:
```python
import jax
import jax.numpy as jnp
from jax import lax
from jax.sharding import PartitionSpec as P


def shards(amps, cycle_inter, k_irrep, i_irrep, j_irrep, virt_count):
    k_local = amps.shape[0]
    slab_size = amps.shape[2]
    width = amps.shape[3]
    n_irrep = virt_count.shape[0]
    j_total = cycle_inter.shape[2]
    irreps = jnp.arange(n_irrep, dtype=jnp.int32)
    slot_pos = jnp.arange(width, dtype=jnp.int32)

    def count_of(labels):
        return jnp.sum(jnp.where(labels[..., None] == irreps, virt_count, 0), axis=-1)

    k_first = lax.axis_index("batch") * k_local
    k_labels = lax.dynamic_slice_in_dim(k_irrep, k_first, k_local)
    c_index = lax.axis_index("grp") * slab_size + jnp.arange(slab_size, dtype=jnp.int32)
    c_labels = c_index // width
    c_live = c_index % width < count_of(c_labels)
    a_labels = jnp.bitwise_xor(
        jnp.bitwise_xor(k_labels[:, None, None], i_irrep[None, :, None]), c_labels[None, None, :]
    )
    amp_mask = c_live[None, None, :, None] & (slot_pos < count_of(a_labels)[..., None])
    masked_amps = jnp.where(amp_mask, amps, jnp.zeros((), amps.dtype))
    b_labels = jnp.bitwise_xor(
        jnp.bitwise_xor(k_labels[:, None, None], c_labels[None, :, None]), j_irrep[None, None, :]
    )
    inter_mask = c_live[None, :, None, None] & (slot_pos < count_of(b_labels)[..., None])
    masked_inter = jnp.where(inter_mask, cycle_inter, jnp.zeros((), cycle_inter.dtype))
    sorted_amps = lax.all_to_all(masked_amps, "grp", split_axis=1, concat_axis=2, tiled=True)
    whole_inter = lax.all_gather(masked_inter, "grp", axis=1, tiled=True)
    i_count = sorted_amps.shape[1]
    i_labels = lax.dynamic_slice_in_dim(i_irrep, lax.axis_index("grp") * i_count, i_count)
    k_source = jnp.bitwise_xor(irreps[None, :], k_labels[:, None])
    amp_blocks = sorted_amps.reshape(k_local, i_count, n_irrep, width, width)
    amp_perm = jnp.take_along_axis(amp_blocks, k_source[:, None, :, None, None], axis=2)
    inter_blocks = whole_inter.reshape(k_local, n_irrep, width, j_total, width)
    inter_perm = jnp.take_along_axis(inter_blocks, k_source[:, :, None, None, None], axis=1)
    products = jnp.einsum(
        "kiqca,kqcjb->iqajb", amp_perm, inter_perm, preferred_element_type=jnp.float32
    )
    i_source = jnp.bitwise_xor(irreps[None, :], i_labels[:, None])
    partial_value = jnp.take_along_axis(products, i_source[:, :, None, None, None], axis=1)
    partial_value = jnp.transpose(partial_value, (0, 3, 1, 2, 4)).reshape(
        i_count, j_total, n_irrep * width, width
    )
    rounded = partial_value.astype(jnp.bfloat16)
    resorted = lax.all_to_all(rounded, "grp", split_axis=2, concat_axis=0, tiled=True)
    return lax.psum_scatter(
        resorted.astype(jnp.float32).astype(jnp.bfloat16), "batch", scatter_dimension=1, tiled=True
    )


def solution(mesh):
    return jax.shard_map(
        shards,
        mesh=mesh,
        in_specs=(P("batch", None, "grp", None), P("batch", "grp", None, None), P(), P(), P(), P()),
        out_specs=P(None, "batch", "grp", None),
        check_vma=False,
    )
```

profile of v0, /device:TPU:2, one launch (start us, length us, event | category | flops | bytes accessed | tf_op | source)
XLA Modules:
  0.0 233.2 jit_solution(9864530524184369395)
XLA Ops:
  6.5 0.0 copy-start
  6.5 0.0 all-gather.2.cloned.1.call-start
  6.6 0.7 dynamic_slice.7
  7.3 0.1 broadcast_xor_fusion.3
  7.4 0.7 select_reduce_fusion.2
  8.1 0.7 broadcast_xor_fusion.1
  8.8 0.8 select_reduce_fusion.1
  9.6 0.1 copy.26
  9.7 1.7 fusion.11
  11.3 0.0 all-gather.2.cloned.1.call-update
  11.4 0.7 broadcast_xor_fusion.2
  12.1 0.1 broadcast_xor_fusion
  12.2 0.8 select_reduce_fusion
  13.0 0.1 copy.27
  13.1 2.3 %fusion.8 = bf16[3,64,16,128]{3,2,0,1:T(8,128)(2,1)} fusion(bf16[3,64,16,128]{3,2,1,0:T(8,128)(2,1)} %param.6, s32[3,64,16]{2,0,1:T(4,128)S(1)} %copy.27, pred[16]{0:T(512)(128)(4,1)S(1)} %fusion.18), kind=kLoop, calls=%fused_computation.12 | loop fusion | flops 1179648 | bytes 1585168 | tf_op jit(solution)/shard_map/jit(_where)/select_n | solution.py:28
  15.4 13.9 %all-to-all-start = ((bf16[3,64,16,128]{3,2,0,1:T(8,128)(2,1)}), bf16[3,64,16,128]{3,2,0,1:T(8,128)(2,1)S(1)}, u32[]{:S(2)}, u32[]{:S(2)}) async-start(bf16[3,64,16,128]{3,2,0,1:T(8,128)(2,1)} %fusion.8), calls=%async_computation | async-start | bytes 1572864 | tf_op jit(solution)/shard_map/all_to_all | solution.py:34
  29.3 0.0 reduce-scatter.2.cloned.1.call-start
  29.3 0.1 fusion.14
  29.4 0.1 reshape.379
  29.5 0.0 copy-done
  29.5 0.6 dynamic_slice.6
  30.1 0.6 fusion.19
  30.8 0.6 compare_and_fusion
  31.4 0.1 fusion.17
  31.5 22.4 %all-to-all-done = bf16[3,64,16,128]{3,2,0,1:T(8,128)(2,1)S(1)} async-done(((bf16[3,64,16,128]{3,2,0,1:T(8,128)(2,1)}), bf16[3,64,16,128]{3,2,0,1:T(8,128)(2,1)S(1)}, u32[]{:S(2)}, u32[]{:S(2)}) %all-to-all-start) | async-done | bytes 786464 | tf_op jit(solution)/shard_map/all_to_all | solution.py:34
  53.9 0.1 copy.29
  54.0 0.8 gather_fusion.2
  54.8 47.8 %all-gather.2.cloned.1.call-done = bf16[3,1024,8,128]{3,2,1,0:T(8,128)(2,1)} async-done(((bf16[3,16,8,128]{3,2,1,0:T(8,128)(2,1)}), bf16[3,1024,8,128]{3,2,1,0:T(8,128)(2,1)}) %all-gather.2.cloned.1.call-update) | async-done | bytes 6291472 | tf_op jit(solution)/shard_map/all_gather | solution.py:35
  102.6 7.4 %gather_fusion.1 = bf16[24,128,8,128]{3,2,1,0:T(8,128)(2,1)} fusion(bf16[3,8,128,8,128]{4,3,2,1,0:T(8,128)(2,1)} %bitcast.40, s32[24]{0:T(128)S(1)} %reshape.379), kind=kCustom, calls=%fused_computation.1 | custom fusion | bytes 12583104 | tf_op jit(solution)/shard_map/jit(take_along_axis)/gather | solution.py:42
  110.0 3.4 %broadcast_select_fusion = bf16[3,8,128,8,128]{4,3,2,1,0:T(8,128)(2,1)S(1)} fusion(bf16[3,8,128,8,128]{4,3,2,1,0:T(8,128)(2,1)} %bitcast.37, pred[3,8]{1,0:T(4,128)(4,1)S(1)} %fusion.17), kind=kLoop, calls=%fused_computation.5 | loop fusion | flops 3145728 | bytes 12582936 | tf_op jit(solution)/shard_map/jit(take_along_axis)/select_n | solution.py:42
  113.4 3.5 %fusion.3 = bf16[8,128,8,128]{1,3,2,0:T(8,128)(2,1)} fusion(bf16[3,8,128,8,128]{4,3,2,1,0:T(8,128)(2,1)S(1)} %broadcast_select_fusion, bf16[3,8,128,128]{3,2,1,0:T(8,128)(2,1)S(1)} %bitcast.42, pred[3,8]{1,0:T(4,128)(4,1)S(1)} %fusion.17), kind=kOutput, calls=%fused_computation.8 | convolution fusion | flops 805699584 | bytes 9175064 | tf_op jit(solution)/shard_map/kiqca,kqcjb->iqajb/dot_general | solution.py:43
  117.0 2.5 %gather_fusion = bf16[8,128,8,128]{1,3,2,0:T(8,128)(2,1)S(1)} fusion(bf16[8,128,8,128]{1,3,2,0:T(8,128)(2,1)} %fusion.3, s32[1024]{0:T(1024)S(1)} %pad_clamp_fusion), kind=kCustom, calls=%fused_computation | custom fusion | bytes 4194336 | tf_op jit(solution)/shard_map/jit(take_along_axis)/gather | solution.py:47
  119.5 2.0 fusion.6
  121.5 3.2 %copy.40 = bf16[1,8,8,128,128]{4,1,3,2,0:T(8,128)(2,1)S(1)} copy(bf16[1,8,8,128,128]{3,4,1,2,0:T(8,128)(2,1)} %fusion.6) | data formatting | bytes 4194304 | tf_op jit(solution)/shard_map/convert_element_type | solution.py:51
  124.7 56.5 %all_to_all.27 = bf16[1,8,1024,128]{3,1,0,2:T(8,128)(2,1)S(1)} all-to-all(bf16[1,8,1024,128]{3,1,0,2:T(8,128)(2,1)S(1)} %bitcast.39), channel_id=1, replica_groups=mesh['batch'=8,'grp'=64] {'grp'}, dimensions={2} | all-to-all | bytes 4194304 | tf_op jit(solution)/shard_map/all_to_all | solution.py:52
  181.3 1.7 copy.34
  182.9 0.0 reduce-scatter.2.cloned.1.call-update
  183.0 43.4 %reduce-scatter.2.cloned.1.call-done = bf16[64,1,16,128]{3,2,0,1:T(8,128)(2,1)} async-done(((bf16[64,8,16,128]{3,2,0,1:T(8,128)(2,1)}), bf16[64,1,16,128]{3,2,0,1:T(8,128)(2,1)}) %reduce-scatter.2.cloned.1.call-update) | async-done | bytes 262160 | tf_op jit(solution)/shard_map/reduce_scatter | solution.py:53
  (3 shorter events, 0.0 us)
Async XLA Ops:
  6.5 23.0 %copy-start = (s32[64]{0:T(128)S(1)}, s32[64]{0:T(128)}, u32[]{:S(2)}) copy-start(s32[64]{0:T(128)} %param.9) | copy-start | bytes 772
  6.5 96.1 %all-gather.2.cloned.1.call-start = ((), (), s32[]{:S(2)}) async-start(), calls=%async_computation.3 | async-start | bytes 6389760 | tf_op jit(solution)/shard_map/all_gather | solution.py:35
  15.4 38.4 %all-to-all-start = ((bf16[3,64,16,128]{3,2,0,1:T(8,128)(2,1)}), bf16[3,64,16,128]{3,2,0,1:T(8,128)(2,1)S(1)}, u32[]{:S(2)}, u32[]{:S(2)}) async-start(bf16[3,64,16,128]{3,2,0,1:T(8,128)(2,1)} %fusion.8), calls=%async_computation | async-start | bytes 1572864 | tf_op jit(solution)/shard_map/all_to_all | solution.py:34
  29.3 197.1 %reduce-scatter.2.cloned.1.call-start = ((), (), s32[]{:S(2)}) async-start(), calls=%async_computation.4 | async-start | bytes 2359296 | tf_op jit(solution)/shard_map/reduce_scatter | solution.py:53
Sparse Core Ops, SparseCore 0:
  11.5 91.0 all-gather.1
  183.1 43.2 reduce-scatter.1
where the time goes:
time: 234 us; the launch traced here: 233 us
  waiting for transfers between devices  114 us (49%)
  blocking collectives  56.5 us (24%)
  local copies, waits for them, and re-layouts  17.3 us (7%)
  other arithmetic  14.8 us (6%)
  starting transfers between devices  13.9 us (6%)
  between operations  13.5 us (6%)
  matrix products  3.53 us (2%)
    all_to_all x1, blocking collectives, shards(): lax.all_to_all(rounded, 'grp', split_axis=2, concat_axis=0, tiled=True)  56.5 us
    all_gather x1, waiting for transfers between devices, shards(): whole_inter = lax.all_gather(masked_inter, 'grp', axis=1, tiled=True)  47.8 us
    reduce_scatter x1, waiting for transfers between devices, shards(): lax.psum_scatter(resorted.astype(jnp.float32).astype(jnp.bfloat16), 'batc...  43.4 us
    all_to_all x1, waiting for transfers between devices, shards(): lax.all_to_all(masked_amps, 'grp', split_axis=1, concat_axis=2, tiled=True)  22.4 us
    all_to_all x1, starting transfers between devices, shards(): lax.all_to_all(masked_amps, 'grp', split_axis=1, concat_axis=2, tiled=True)  13.9 us
    gather x2, local copies, waits for them, and re-layouts, shards(): jnp.take_along_axis(inter_blocks, k_source[:, :, None, None, None], axis=1)  7.46 us
  transfers between devices with their start and end apart: 3, of which 3 were waited for; matrix products, arithmetic and copies ran while one was open for 3% of the time, Pallas kernels for 0%

commit v1 on v0

--- a/solution.py
+++ b/solution.py
@@ -32,7 +32,9 @@
     inter_mask = c_live[None, :, None, None] & (slot_pos < count_of(b_labels)[..., None])
     masked_inter = jnp.where(inter_mask, cycle_inter, jnp.zeros((), cycle_inter.dtype))
     sorted_amps = lax.all_to_all(masked_amps, "grp", split_axis=1, concat_axis=2, tiled=True)
-    whole_inter = lax.all_gather(masked_inter, "grp", axis=1, tiled=True)
+    whole_inter = jnp.concatenate(
+        lax.all_to_all(jnp.stack([masked_inter] * lax.axis_size("grp")), "grp", 0, 0), axis=1
+    )
     i_count = sorted_amps.shape[1]
     i_labels = lax.dynamic_slice_in_dim(i_irrep, lax.axis_index("grp") * i_count, i_count)
     k_source = jnp.bitwise_xor(irreps[None, :], k_labels[:, None])

time: 234 us -> 339 us (1.45)
  the two profiles are of different devices: /device:TPU:2 before, /device:TPU:4 now
where the time goes in v1:
time: 339 us; the launch traced here: 338 us
  waiting for transfers between devices  198 us (58%)
  blocking collectives  57.5 us (17%)
  local copies, waits for them, and re-layouts  29.6 us (9%)
  starting transfers between devices  21.5 us (6%)
  other arithmetic  14.2 us (4%)
  between operations  13.5 us (4%)
  matrix products  3.53 us (1%)
    all_to_all x1, waiting for transfers between devices, shards(): lax.all_to_all(jnp.stack([masked_inter] * lax.axis_size('grp')), 'grp', 0...  134 us
    all_to_all x1, blocking collectives, shards(): lax.all_to_all(rounded, 'grp', split_axis=2, concat_axis=0, tiled=True)  57.5 us
    reduce_scatter x1, waiting for transfers between devices, shards(): lax.psum_scatter(resorted.astype(jnp.float32).astype(jnp.bfloat16), 'batc...  44.4 us
    all_to_all x1, waiting for transfers between devices, shards(): lax.all_to_all(masked_amps, 'grp', split_axis=1, concat_axis=2, tiled=True)  19.2 us
    all_to_all x1, starting transfers between devices, shards(): lax.all_to_all(masked_amps, 'grp', split_axis=1, concat_axis=2, tiled=True)  13.9 us
    all_to_all x1, local copies, waits for them, and re-layouts, shards(): lax.all_to_all(jnp.stack([masked_inter] * lax.axis_size('grp')), 'grp', 0...  8.08 us
    all_to_all x1, starting transfers between devices, shards(): lax.all_to_all(jnp.stack([masked_inter] * lax.axis_size('grp')), 'grp', 0...  7.54 us
    gather x2, local copies, waits for them, and re-layouts, shards(): jnp.take_along_axis(inter_blocks, k_source[:, :, None, None, None], axis=1)  7.46 us
  transfers between devices with their start and end apart: 3, of which 3 were waited for; matrix products, arithmetic and copies ran while one was open for 2% of the time, Pallas kernels for 0%

profile of v1, /device:TPU:4, one launch (start us, length us, event | category | flops | bytes accessed | tf_op | source)
XLA Modules:
  0.0 337.9 jit_solution(15253907489876671811)
XLA Ops:
  6.5 0.7 select_reduce_fusion.2
  7.3 0.7 dynamic_slice.7
  8.0 0.7 broadcast_xor_fusion.2
  8.8 0.1 broadcast_xor_fusion
  8.8 0.8 select_reduce_fusion
  9.6 0.1 copy.30
  9.7 2.4 fusion.8
  12.1 13.9 %all-to-all-start.1 = ((bf16[3,64,16,128]{3,2,0,1:T(8,128)(2,1)}), bf16[3,64,16,128]{3,2,0,1:T(8,128)(2,1)S(1)}, u32[]{:S(2)}, u32[]{:S(2)}) async-start(bf16[3,64,16,128]{3,2,0,1:T(8,128)(2,1)} %fusion.8), calls=%async_computation.1 | async-start | bytes 1572864 | tf_op jit(solution)/shard_map/all_to_all | solution.py:34
  26.0 0.1 broadcast_xor_fusion.3
  26.1 0.7 broadcast_xor_fusion.1
  26.8 0.8 select_reduce_fusion.1
  27.6 0.1 copy.28
  27.7 1.0 fusion.11
  28.7 19.2 %all-to-all-done.1 = bf16[3,64,16,128]{3,2,0,1:T(8,128)(2,1)S(1)} async-done(((bf16[3,64,16,128]{3,2,0,1:T(8,128)(2,1)}), bf16[3,64,16,128]{3,2,0,1:T(8,128)(2,1)S(1)}, u32[]{:S(2)}, u32[]{:S(2)}) %all-to-all-start.1) | async-done | bytes 786464 | tf_op jit(solution)/shard_map/all_to_all | solution.py:34
  47.9 4.2 %stack.2 = bf16[64,3,16,8,128]{4,3,2,1,0:T(8,128)(2,1)} broadcast(bf16[3,16,8,128]{3,2,1,0:T(8,128)(2,1)S(1)} %fusion.11), dimensions={1,2,3,4} | broadcast | bytes 6389760 | tf_op jit(solution)/shard_map/stack | solution.py:36
  52.2 0.0 copy-start
  52.2 7.5 %all-to-all-start = ((bf16[64,3,16,8,128]{4,3,2,1,0:T(8,128)(2,1)}), bf16[64,3,16,8,128]{4,3,2,1,0:T(8,128)(2,1)}, u32[]{:S(2)}, u32[]{:S(2)}) async-start(bf16[64,3,16,8,128]{4,3,2,1,0:T(8,128)(2,1)} %stack.2), calls=%async_computation | async-start | bytes 12582912 | tf_op jit(solution)/shard_map/all_to_all | solution.py:36
  59.7 0.0 reduce-scatter.2.cloned.1.call-start
  59.8 0.1 fusion.14
  59.9 0.1 reshape.381
  59.9 0.0 copy-done
  59.9 0.6 dynamic_slice.6
  60.5 0.6 fusion.19
  61.2 0.7 compare_and_fusion
  61.9 0.1 fusion.17
  61.9 0.1 copy.32
  62.1 0.8 gather_fusion.2
  62.8 134.3 %all-to-all-done = bf16[64,3,16,8,128]{4,3,2,1,0:T(8,128)(2,1)} async-done(((bf16[64,3,16,8,128]{4,3,2,1,0:T(8,128)(2,1)}), bf16[64,3,16,8,128]{4,3,2,1,0:T(8,128)(2,1)}, u32[]{:S(2)}, u32[]{:S(2)}) %all-to-all-start) | async-done | bytes 6291488 | tf_op jit(solution)/shard_map/all_to_all | solution.py:36
  197.2 8.1 %copy.29 = bf16[64,3,16,8,128]{4,3,2,0,1:T(8,128)(2,1)} copy(bf16[64,3,16,8,128]{4,3,2,1,0:T(8,128)(2,1)} %all-to-all-done) | data formatting | bytes 12582912 | tf_op jit(solution)/shard_map/all_to_all | solution.py:36
  205.3 7.4 %gather_fusion.1 = bf16[24,128,8,128]{3,2,1,0:T(8,128)(2,1)} fusion(bf16[3,8,128,8,128]{4,3,2,1,0:T(8,128)(2,1)} %bitcast.39, s32[24]{0:T(128)S(1)} %reshape.381), kind=kCustom, calls=%fused_computation.1 | custom fusion | bytes 12583104 | tf_op jit(solution)/shard_map/jit(take_along_axis)/gather | solution.py:44
  212.6 3.4 %broadcast_select_fusion = bf16[3,8,128,8,128]{4,3,2,1,0:T(8,128)(2,1)S(1)} fusion(bf16[3,8,128,8,128]{4,3,2,1,0:T(8,128)(2,1)} %bitcast.40, pred[3,8]{1,0:T(4,128)(4,1)S(1)} %fusion.17), kind=kLoop, calls=%fused_computation.5 | loop fusion | flops 3145728 | bytes 12582936 | tf_op jit(solution)/shard_map/jit(take_along_axis)/select_n | solution.py:44
  216.1 3.5 %fusion.3 = bf16[8,128,8,128]{1,3,2,0:T(8,128)(2,1)} fusion(bf16[3,8,128,8,128]{4,3,2,1,0:T(8,128)(2,1)S(1)} %broadcast_select_fusion, bf16[3,8,128,128]{3,2,1,0:T(8,128)(2,1)S(1)} %bitcast.44, pred[3,8]{1,0:T(4,128)(4,1)S(1)} %fusion.17), kind=kOutput, calls=%fused_computation.8 | convolution fusion | flops 805699584 | bytes 9175064 | tf_op jit(solution)/shard_map/kiqca,kqcjb->iqajb/dot_general | solution.py:45
  219.6 2.5 gather_fusion
  222.2 2.0 fusion.6
  224.2 3.2 copy.43
  227.4 57.5 %all_to_all.32 = bf16[1,8,1024,128]{3,1,0,2:T(8,128)(2,1)S(1)} all-to-all(bf16[1,8,1024,128]{3,1,0,2:T(8,128)(2,1)S(1)} %bitcast.42), channel_id=1, replica_groups=mesh['batch'=8,'grp'=64] {'grp'}, dimensions={2} | all-to-all | bytes 4194304 | tf_op jit(solution)/shard_map/all_to_all | solution.py:54
  285.0 1.7 copy.37
  286.7 0.0 reduce-scatter.2.cloned.1.call-update
  286.7 44.4 %reduce-scatter.2.cloned.1.call-done = bf16[64,1,16,128]{3,2,0,1:T(8,128)(2,1)} async-done(((bf16[64,8,16,128]{3,2,0,1:T(8,128)(2,1)}), bf16[64,1,16,128]{3,2,0,1:T(8,128)(2,1)}) %reduce-scatter.2.cloned.1.call-update) | async-done | bytes 262160 | tf_op jit(solution)/shard_map/reduce_scatter | solution.py:55
  (3 shorter events, 0.0 us)
Async XLA Ops:
  12.1 35.8 %all-to-all-start.1 = ((bf16[3,64,16,128]{3,2,0,1:T(8,128)(2,1)}), bf16[3,64,16,128]{3,2,0,1:T(8,128)(2,1)S(1)}, u32[]{:S(2)}, u32[]{:S(2)}) async-start(bf16[3,64,16,128]{3,2,0,1:T(8,128)(2,1)} %fusion.8), calls=%async_computation.1 | async-start | bytes 1572864 | tf_op jit(solution)/shard_map/all_to_all | solution.py:34
  52.2 7.8 %copy-start = (s32[64]{0:T(128)S(1)}, s32[64]{0:T(128)}, u32[]{:S(2)}) copy-start(s32[64]{0:T(128)} %param.9) | copy-start | bytes 772
  52.2 145.0 %all-to-all-start = ((bf16[64,3,16,8,128]{4,3,2,1,0:T(8,128)(2,1)}), bf16[64,3,16,8,128]{4,3,2,1,0:T(8,128)(2,1)}, u32[]{:S(2)}, u32[]{:S(2)}) async-start(bf16[64,3,16,8,128]{4,3,2,1,0:T(8,128)(2,1)} %stack.2), calls=%async_computation | async-start | bytes 12582912 | tf_op jit(solution)/shard_map/all_to_all | solution.py:36
  59.7 271.4 %reduce-scatter.2.cloned.1.call-start = ((), (), s32[]{:S(2)}) async-start(), calls=%async_computation.4 | async-start | bytes 2359296 | tf_op jit(solution)/shard_map/reduce_scatter | solution.py:55
Sparse Core Ops, SparseCore 0:
  286.8 44.2 reduce-scatter.1
